TPU v7x, 32 devices: a whole 2x2x4 slice. The times are simulated.
32 devices in a mesh: sec: 2 (over x), blk: 8 (over z, y), mp: 2 (over core).
Axes of the slice: x: 2, y: 2, z: 4, core: 2. Of those that a mesh axis runs over, the one named last changes fastest.
Arguments:
- image_pooled: bfloat16 [1536, 1536], P('blk', ('sec', 'mp')), may hold values from -4 to 4
- text_pooled: bfloat16 [1536, 2048], P('blk', ('sec', 'mp')), may hold values from -4 to 4
- image_proj: bfloat16 [1536, 1152], P(('sec', 'mp')), may hold values from -0.15625 to 0.15625
- text_proj: bfloat16 [2048, 1152], P(('sec', 'mp')), may hold values from -0.125 to 0.125
- natural_log_multiplier: float32 [1], replicated, may hold values from 1.4 to 2.3
- logit_bias: float32 [1], replicated, may hold values from -2 to -0.5
- match_cluster_labels: int32 [1536], P('blk'), may hold values from 0 to 1535
Outputs:
- pair_loss: float32 [2, 1536], P('sec', 'blk')
- image_grad: bfloat16 [1536, 1536], P('blk', ('sec', 'mp'))
- text_grad: bfloat16 [1536, 2048], P('blk', ('sec', 'mp'))
All inputs are finite; a program needn't handle non-finite values.
Results may differ from a plain program's by a relative error of at most 0.0065.
Values may be sent and summed in bfloat16 or wider, within the bound.
No kernel may reach another device: no remote copies, remote signals or barrier semaphores. Data moves between devices by JAX's collectives and lax.ppermute only.
A program may use at most 128 MiB of HBM per device.

v0:
```python
import jax
import jax.numpy as jnp
from jax import lax
from jax.sharding import PartitionSpec as P


def unit_rows(embedding):
    row_norm = jnp.sqrt(jnp.sum(embedding * embedding, axis=1, keepdims=True) + 1e-06)
    return (embedding / row_norm, row_norm)


def per_device(
    image_pooled,
    text_pooled,
    image_proj,
    text_proj,
    natural_log_multiplier,
    logit_bias,
    match_cluster_labels,
):
    part_image = jnp.dot(image_pooled, image_proj, preferred_element_type=jnp.float32)
    part_text = jnp.dot(text_pooled, text_proj, preferred_element_type=jnp.float32)
    stacked = jnp.stack([part_image, part_text])
    section = lax.axis_index("sec")
    both_sums = lax.psum(stacked, ("sec", "mp"))
    own_emb = lax.dynamic_index_in_dim(both_sums, section, 0, keepdims=False)
    other_emb = lax.dynamic_index_in_dim(both_sums, 1 - section, 0, keepdims=False)
    own_unit, own_norm = unit_rows(own_emb)
    resident_slice = own_unit.astype(jnp.bfloat16)
    other_unit, other_norm = unit_rows(other_emb)
    counterpart_slice = other_unit.astype(jnp.bfloat16)
    sharpness_factor = jnp.exp(natural_log_multiplier[0])
    shift_quantity = logit_bias[0]
    visit_rows = lax.all_gather(counterpart_slice, "blk", axis=0, tiled=True)
    visited_ids = lax.all_gather(match_cluster_labels, "blk", axis=0, tiled=True)
    agreement_scores_matrix = (
        sharpness_factor
        * lax.dot_general(
            resident_slice, visit_rows, (((1,), (1,)), ((), ())), preferred_element_type=jnp.float32
        )
        + shift_quantity
    )
    desired_polarity = jnp.where(
        match_cluster_labels[:, None] == visited_ids[None, :], 1.0, -1.0
    ).astype(jnp.float32)
    row_losses = jnp.sum(jax.nn.softplus(-desired_polarity * agreement_scores_matrix), axis=1)
    penalty_factor = (
        -sharpness_factor
        * desired_polarity
        * jax.nn.sigmoid(-desired_polarity * agreement_scores_matrix)
    ).astype(jnp.bfloat16)
    unit_grad = jnp.dot(penalty_factor, visit_rows, preferred_element_type=jnp.float32)
    unit_grad, row_losses = (unit_grad, row_losses)
    projection = jnp.sum(own_unit * unit_grad, axis=1, keepdims=True)
    own_demb = ((unit_grad - own_unit * projection) / own_norm).astype(jnp.bfloat16)
    both_grads = lax.all_gather(own_demb[None], "sec", axis=0, tiled=True)
    image_grad = lax.dot_general(
        both_grads[0], image_proj, (((1,), (1,)), ((), ())), preferred_element_type=jnp.float32
    ).astype(jnp.bfloat16)
    text_grad = lax.dot_general(
        both_grads[1], text_proj, (((1,), (1,)), ((), ())), preferred_element_type=jnp.float32
    ).astype(jnp.bfloat16)
    return (row_losses[None, :], image_grad, text_grad)


def solution(mesh):
    placed = (
        P("blk", ("sec", "mp")),
        P("blk", ("sec", "mp")),
        P(("sec", "mp"), None),
        P(("sec", "mp"), None),
        P(),
        P(),
        P("blk"),
    )
    return jax.shard_map(
        per_device,
        mesh=mesh,
        in_specs=placed,
        out_specs=(P("sec", "blk"), P("blk", ("sec", "mp")), P("blk", ("sec", "mp"))),
        check_vma=False,
    )
```

profile of v0, /device:TPU:0, one launch (start us, length us, event | category | flops | bytes accessed | tf_op | source)
XLA Modules:
  0.0 155.9 jit_solution(17890607806463199969)
XLA Ops:
  7.2 0.0 copy-start
  7.2 0.0 copy-start.4
  7.2 0.0 copy-start.2
  7.2 0.0 all-reduce.3.cloned.1.call-start
  7.2 1.2 copy-done
  8.4 1.4 convolution_bitcast_fusion
  9.8 0.0 copy-done.4
  9.8 0.0 copy-done.2
  9.8 0.4 convolution_bitcast_fusion.1
  10.2 1.3 pad_maximum_fusion
  11.6 0.0 all-reduce.3.cloned.1.call-update
  11.6 0.0 all-gather.3.cloned.1.call-start
  11.6 48.8 %all-reduce.3.cloned.1.call-done = f32[2,192,1152]{2,1,0:T(8,128)} async-done(((f32[2,192,1152]{2,1,0:T(8,128)}), f32[2,192,1152]{2,1,0:T(8,128)}) %all-reduce.3.cloned.1.call-update) | async-done | bytes 1769488 | tf_op jit(solution)/shard_map/psum | solution.py:25
  60.5 0.0 copy-start.1
  60.5 1.8 %fusion.7 = (f32[192]{0:T(256)S(1)}, f32[192]{0:T(256)S(1)}) fusion(f32[2,192,1152]{2,1,0:T(8,128)} %all-reduce.3.cloned.1.call-done, s32[]{:T(128)S(6)} %select_n.16, s32[]{:T(128)S(6)} %select_n.17), kind=kLoop, calls=%fused_computation.20 | loop fusion | flops 884352 | bytes 1771016 | tf_op jit(solution)/shard_map/reduce_sum | solution.py:8
  62.2 0.0 copy-start.7
  62.3 0.0 copy-start.5
  62.3 0.2 copy-done.1
  62.5 0.9 fusion.6
  63.4 0.0 all-gather.3.cloned.1.call-update
  64.7 0.0 copy-done.7
  64.8 0.6 dynamic-slice
  66.0 0.0 copy-done.5
  66.0 0.3 dynamic-update-slice
  66.3 12.1 %all-reduce = s32[1536]{0:T(1024)S(1)} all-reduce(s32[1536]{0:T(1024)S(1)} %dynamic-update-slice), channel_id=1, replica_groups=mesh['sec'=2,'blk'=8,'mp'=2] {'blk'}, use_global_device_ids=true, to_apply=%add | all-reduce | flops 1536 | bytes 12288
  78.4 50.5 %all-gather.3.cloned.1.call-done = bf16[1536,1152]{1,0:T(8,128)(2,1)} async-done(((bf16[192,1152]{1,0:T(8,128)(2,1)}), bf16[1536,1152]{1,0:T(8,128)(2,1)}) %all-gather.3.cloned.1.call-update) | async-done | bytes 3538960 | tf_op jit(solution)/shard_map/all_gather | solution.py:34
  128.9 0.0 copy-start.6
  128.9 4.7 %fusion.4 = (f32[192]{0:T(256)}, f32[192,1536]{1,0:T(8,128)S(1)}) fusion(f32[]{:T(128)} %bitcast.37, bf16[1536,1152]{1,0:T(8,128)(2,1)} %all-gather.3.cloned.1.call-done, f32[192]{0:T(256)S(1)} %add_sqrt_fusion.1, f32[2,192,1152]{2,1,0:T(8,128)S(1)} %copy-done.1, s32[]{:T(128)S(6)} %select_n.16, f32[]{:T(128)} %bitcast.1, s32[1536]{0:T(1024)S(1)} %all-reduce, ...), kind=kOutput, calls=%fused_computation.11 | convolution fusion | flops 683753280 | bytes 5614348 | tf_op jit(solution)/shard_map/dot_general | solution.py:38
  133.6 0.0 copy-done.6
  133.6 1.1 multiply_reduce_fusion
  134.7 0.2 divide_convert_fusion
  135.0 0.0 copy-start.3
  135.0 11.7 %all-gather = bf16[384,1152]{1,0:T(8,128)(2,1)S(1)} all-gather(bf16[192,1152]{1,0:T(8,128)(2,1)S(1)} %divide_convert_fusion), channel_id=2, replica_groups=mesh['sec'=2,'blk'=8,'mp'=2] {'sec'}, dimensions={0}, use_global_device_ids=true | all-gather | bytes 1327104 | tf_op jit(solution)/shard_map/all_gather | solution.py:56
  146.7 0.0 copy-done.3
  146.7 1.1 convolution_convert_fusion.1
  147.8 1.2 convolution_convert_fusion
  (3 shorter events, 0.0 us)
Async XLA Ops:
  7.2 1.3 copy-start
  7.2 2.6 %copy-start.4 = (bf16[192,384]{1,0:T(8,128)(2,1)S(1)}, bf16[192,384]{1,0:T(8,128)(2,1)}, u32[]{:S(2)}) copy-start(bf16[192,384]{1,0:T(8,128)(2,1)} %param.7) | copy-start | bytes 442372
  7.2 2.6 %copy-start.2 = (bf16[384,1152]{1,0:T(8,128)(2,1)S(1)}, bf16[384,1152]{1,0:T(8,128)(2,1)}, u32[]{:S(2)}) copy-start(bf16[384,1152]{1,0:T(8,128)(2,1)} %param.9) | copy-start | bytes 2654212
  7.2 53.3 %all-reduce.3.cloned.1.call-start = ((), (), s32[]{:S(2)}) async-start(), calls=%async_computation | async-start | bytes 3538944 | tf_op jit(solution)/shard_map/psum | solution.py:25
  11.6 117.3 %all-gather.3.cloned.1.call-start = ((), (), s32[]{:S(2)}) async-start(), calls=%async_computation.1 | async-start | bytes 3981312 | tf_op jit(solution)/shard_map/all_gather | solution.py:34
  60.5 2.0 %copy-start.1 = (f32[2,192,1152]{2,1,0:T(8,128)S(1)}, f32[2,192,1152]{2,1,0:T(8,128)}, u32[]{:S(2)}) copy-start(f32[2,192,1152]{2,1,0:T(8,128)} %all-reduce.3.cloned.1.call-done) | copy-start | bytes 5308420
  62.2 2.5 %copy-start.7 = (u32[32]{0:T(128)S(1)}, u32[32]{0:T(128)}, u32[]{:S(2)}) copy-start(u32[32]{0:T(128)} %constant.31) | copy-start | bytes 388
  62.3 3.8 %copy-start.5 = (s32[192]{0:T(256)S(1)}, s32[192]{0:T(256)}, u32[]{:S(2)}) copy-start(s32[192]{0:T(256)} %param.13) | copy-start | bytes 2308
  128.9 4.7 %copy-start.6 = (bf16[1536,1152]{1,0:T(8,128)(2,1)S(1)}, bf16[1536,1152]{1,0:T(8,128)(2,1)}, u32[]{:S(2)}) copy-start(bf16[1536,1152]{1,0:T(8,128)(2,1)} %all-gather.3.cloned.1.call-done) | copy-start | bytes 10616836
  135.0 11.8 %copy-start.3 = (bf16[384,1152]{1,0:T(8,128)(2,1)S(1)}, bf16[384,1152]{1,0:T(8,128)(2,1)}, u32[]{:S(2)}) copy-start(bf16[384,1152]{1,0:T(8,128)(2,1)} %param.9) | copy-start | bytes 2654212
Sparse Core Ops, SparseCore 0:
  11.7 48.7 all-reduce.2
  63.5 65.3 all-gather.2
where the time goes:
time: 156 us
  waiting for transfers between devices  99.4 us (64%)
  blocking collectives  23.8 us (15%)
  between operations  16.2 us (10%)
  matrix products  9.9 us (6%)
  other arithmetic  4.2 us (3%)
  local copies, waits for them, and re-layouts  2.31 us (1%)
    all_gather x1, waiting for transfers between devices, per_device(): visit_rows = lax.all_gather(counterpart_slice, 'blk', axis=0, tiled=True)  50.5 us
    psum x1, waiting for transfers between devices, per_device(): both_sums = lax.psum(stacked, ('sec', 'mp'))  48.8 us
    unnamed x1, blocking collectives  12.1 us
    all_gather x1, blocking collectives, per_device(): both_grads = lax.all_gather(own_demb[None], 'sec', axis=0, tiled=True)  11.7 us
    dot_general x1, matrix products, per_device(): lax.dot_general(resident_slice, visit_rows, (((1,), (1,)), ((), ())), pre...  4.68 us
  transfers between devices with their start and end apart: 2, of which 2 were waited for; matrix products, arithmetic and copies ran while one was open for 1% of the time, Pallas kernels for 0%

commit v1 on v0

--- a/solution.py
+++ b/solution.py
@@ -22,7 +22,8 @@
     part_text = jnp.dot(text_pooled, text_proj, preferred_element_type=jnp.float32)
     stacked = jnp.stack([part_image, part_text])
     section = lax.axis_index("sec")
-    both_sums = lax.psum(stacked, ("sec", "mp"))
+    parts = lax.all_gather(stacked, ("sec", "mp"))
+    both_sums = jnp.sum(parts, axis=0)
     own_emb = lax.dynamic_index_in_dim(both_sums, section, 0, keepdims=False)
     other_emb = lax.dynamic_index_in_dim(both_sums, 1 - section, 0, keepdims=False)
     own_unit, own_norm = unit_rows(own_emb)

time: 156 us -> 163 us (1.045)
  waiting for transfers between devices: 99.4 us -> 104 us
  other arithmetic: 4.2 us -> 6.33 us
    all_gather x0 -> x1, waiting for transfers between devices: none -> 53.6 us  [per_device(): parts = lax.all_gather(stacked, ('sec', 'mp'))]
    psum x1 -> x0, waiting for transfers between devices: 48.8 us -> none  [per_device(): both_sums = lax.psum(stacked, ('sec', 'mp'))]
    reduce_sum x0 -> x1, other arithmetic: none -> 3.58 us  [per_device(): both_sums = jnp.sum(parts, axis=0)]
where the time goes in v1:
time: 163 us
  waiting for transfers between devices  104 us (64%)
  blocking collectives  23.8 us (15%)
  between operations  16.2 us (10%)
  matrix products  9.9 us (6%)
  other arithmetic  6.33 us (4%)
  local copies, waits for them, and re-layouts  2.1 us (1%)
    all_gather x1, waiting for transfers between devices, per_device(): parts = lax.all_gather(stacked, ('sec', 'mp'))  53.6 us
    all_gather x1, waiting for transfers between devices, per_device(): visit_rows = lax.all_gather(counterpart_slice, 'blk', axis=0, tiled=True)  50.5 us
    unnamed x1, blocking collectives  12.1 us
    all_gather x1, blocking collectives, per_device(): both_grads = lax.all_gather(own_demb[None], 'sec', axis=0, tiled=True)  11.7 us
    dot_general x1, matrix products, per_device(): lax.dot_general(resident_slice, visit_rows, (((1,), (1,)), ((), ())), pre...  4.68 us
    reduce_sum x1, other arithmetic, per_device(): both_sums = jnp.sum(parts, axis=0)  3.58 us
  transfers between devices with their start and end apart: 2, of which 2 were waited for; matrix products, arithmetic and copies ran while one was open for 1% of the time, Pallas kernels for 0%

profile of v1, /device:TPU:0, one launch (start us, length us, event | category | flops | bytes accessed | tf_op | source)
XLA Modules:
  0.0 162.5 jit_solution(6707643929582511665)
XLA Ops:
  7.2 0.0 copy-start
  7.2 0.0 copy-start.3
  7.2 0.0 copy-start.1
  7.2 0.0 all-gather.7.cloned.1.call-start
  7.2 1.2 copy-done
  8.4 1.4 convolution_bitcast_fusion
  9.8 0.0 copy-done.3
  9.8 0.0 copy-done.1
  9.8 0.4 convolution_bitcast_fusion.1
  10.2 1.4 pad_maximum_fusion
  11.6 0.0 all-gather.7.cloned.1.call-update
  11.7 0.0 all-gather.5.cloned.1.call-start
  11.7 53.6 %all-gather.7.cloned.1.call-done = f32[8,192,1152]{2,1,0:T(8,128)} async-done(((f32[2,192,1152]{2,1,0:T(8,128)}), f32[8,192,1152]{2,1,0:T(8,128)}) %all-gather.7.cloned.1.call-update) | async-done | bytes 7077904 | tf_op jit(solution)/shard_map/all_gather | solution.py:25
  65.4 3.6 %reduce_sum.45 = f32[2,192,1152]{2,1,0:T(8,128)S(1)} reduce(f32[4,2,192,1152]{3,2,1,0:T(8,128)} %bitcast.39, f32[]{:T(128)} %constant.12.clone.1), dimensions={0}, to_apply=%region_0.0 | reduce | flops 1327104 | bytes 8847364 | tf_op jit(solution)/shard_map/reduce_sum | solution.py:26
  69.0 0.2 fusion.7
  69.2 0.0 copy-start.6
  69.2 0.0 copy-start.4
  69.2 0.9 fusion.6
  70.1 0.0 all-gather.5.cloned.1.call-update
  71.4 0.0 copy-done.6
  71.5 0.6 dynamic-slice
  72.7 0.0 copy-done.4
  72.7 0.3 dynamic-update-slice
  73.0 12.1 %all-reduce = s32[1536]{0:T(1024)S(1)} all-reduce(s32[1536]{0:T(1024)S(1)} %dynamic-update-slice), channel_id=1, replica_groups=mesh['sec'=2,'blk'=8,'mp'=2] {'blk'}, use_global_device_ids=true, to_apply=%add | all-reduce | flops 1536 | bytes 12288
  85.1 50.5 %all-gather.5.cloned.1.call-done = bf16[1536,1152]{1,0:T(8,128)(2,1)} async-done(((bf16[192,1152]{1,0:T(8,128)(2,1)}), bf16[1536,1152]{1,0:T(8,128)(2,1)}) %all-gather.5.cloned.1.call-update) | async-done | bytes 3538960 | tf_op jit(solution)/shard_map/all_gather | solution.py:35
  135.6 0.0 copy-start.5
  135.6 4.7 %fusion.4 = (f32[192]{0:T(256)}, f32[192,1536]{1,0:T(8,128)S(1)}) fusion(f32[]{:T(128)} %bitcast.38, bf16[1536,1152]{1,0:T(8,128)(2,1)} %all-gather.5.cloned.1.call-done, f32[192]{0:T(256)S(1)} %add_sqrt_fusion.1, f32[2,192,1152]{2,1,0:T(8,128)S(1)} %reduce_sum.45, s32[]{:T(128)S(6)} %select_n.16, f32[]{:T(128)} %bitcast.1, s32[1536]{0:T(1024)S(1)} %all-reduce, ...), kind=kOutput, calls=%fused_computation.11 | convolution fusion | flops 683753280 | bytes 5614348 | tf_op jit(solution)/shard_map/dot_general | solution.py:39
  140.2 0.0 copy-done.5
  140.2 1.1 multiply_reduce_fusion
  141.4 0.2 divide_convert_fusion
  141.6 0.0 copy-start.2
  141.6 11.7 %all-gather.1 = bf16[384,1152]{1,0:T(8,128)(2,1)S(1)} all-gather(bf16[192,1152]{1,0:T(8,128)(2,1)S(1)} %divide_convert_fusion), channel_id=3, replica_groups=mesh['sec'=2,'blk'=8,'mp'=2] {'sec'}, dimensions={0}, use_global_device_ids=true | all-gather | bytes 1327104 | tf_op jit(solution)/shard_map/all_gather | solution.py:57
  153.4 0.0 copy-done.2
  153.4 1.1 convolution_convert_fusion.1
  154.5 1.2 convolution_convert_fusion
  (3 shorter events, 0.0 us)
Async XLA Ops:
  7.2 1.3 copy-start
  7.2 2.6 %copy-start.3 = (bf16[192,384]{1,0:T(8,128)(2,1)S(1)}, bf16[192,384]{1,0:T(8,128)(2,1)}, u32[]{:S(2)}) copy-start(bf16[192,384]{1,0:T(8,128)(2,1)} %param.7) | copy-start | bytes 442372
  7.2 2.6 %copy-start.1 = (bf16[384,1152]{1,0:T(8,128)(2,1)S(1)}, bf16[384,1152]{1,0:T(8,128)(2,1)}, u32[]{:S(2)}) copy-start(bf16[384,1152]{1,0:T(8,128)(2,1)} %param.9) | copy-start | bytes 2654212
  7.2 58.2 %all-gather.7.cloned.1.call-start = ((), (), s32[]{:S(2)}) async-start(), calls=%async_computation.1 | async-start | bytes 8847360 | tf_op jit(solution)/shard_map/all_gather | solution.py:25
  11.7 123.9 %all-gather.5.cloned.1.call-start = ((), (), s32[]{:S(2)}) async-start(), calls=%async_computation | async-start | bytes 3981312 | tf_op jit(solution)/shard_map/all_gather | solution.py:35
  69.2 2.3 %copy-start.6 = (u32[32]{0:T(128)S(1)}, u32[32]{0:T(128)}, u32[]{:S(2)}) copy-start(u32[32]{0:T(128)} %constant.31) | copy-start | bytes 388
  69.2 3.5 %copy-start.4 = (s32[192]{0:T(256)S(1)}, s32[192]{0:T(256)}, u32[]{:S(2)}) copy-start(s32[192]{0:T(256)} %param.13) | copy-start | bytes 2308
  135.6 4.7 %copy-start.5 = (bf16[1536,1152]{1,0:T(8,128)(2,1)S(1)}, bf16[1536,1152]{1,0:T(8,128)(2,1)}, u32[]{:S(2)}) copy-start(bf16[1536,1152]{1,0:T(8,128)(2,1)} %all-gather.5.cloned.1.call-done) | copy-start | bytes 10616836
  141.6 11.8 %copy-start.2 = (bf16[384,1152]{1,0:T(8,128)(2,1)S(1)}, bf16[384,1152]{1,0:T(8,128)(2,1)}, u32[]{:S(2)}) copy-start(bf16[384,1152]{1,0:T(8,128)(2,1)} %param.9) | copy-start | bytes 2654212
Sparse Core Ops, SparseCore 0:
  11.8 53.5 all-gather.6
  70.2 65.2 all-gather.4
